TPU v7x, 32 devices: a whole 2x2x4 slice. The times are simulated.
32 devices in a mesh: items: 8 (over y, x, core), seq: 4 (over z).
Axes of the slice: x: 2, y: 2, z: 4, core: 2. Of those that a mesh axis runs over, the one named last changes fastest.
Arguments:
- tokens: bfloat16 [24, 400, 768], P('items', 'seq'), may hold values from -6 to 6
- cotangent: bfloat16 [24, 400, 768], P('items', 'seq'), may hold values from -6 to 6
- ln1_gain: bfloat16 [768], replicated, may hold values from 0.099609375 to 1.8984375
- ln1_shift: bfloat16 [768], replicated, may hold values from -3 to 3
- w_query: bfloat16 [768, 768], replicated, may hold values from -0.21875 to 0.21875
- b_query: bfloat16 [768], replicated, may hold values from -3 to 3
- w_key: bfloat16 [768, 768], replicated, may hold values from -0.21875 to 0.21875
- w_value: bfloat16 [768, 768], replicated, may hold values from -0.21875 to 0.21875
- b_value: bfloat16 [768], replicated, may hold values from -3 to 3
- w_out: bfloat16 [768, 768], replicated, may hold values from -3.5 to 3.5
- b_out: bfloat16 [768], replicated, may hold values from -3 to 3
- ln2_gain: bfloat16 [768], replicated, may hold values from 0.099609375 to 1.8984375
- ln2_shift: bfloat16 [768], replicated, may hold values from -3 to 3
- w_inner: bfloat16 [768, 3072], replicated, may hold values from -0.21875 to 0.21875
- b_inner: bfloat16 [3072], replicated, may hold values from -3 to 3
- w_outer: bfloat16 [3072, 768], replicated, may hold values from -0.109375 to 0.109375
- b_outer: bfloat16 [768], replicated, may hold values from -3 to 3
- key_valid: int32 [24, 400], P('items'), may hold values from 0 to 1, as said below
Outputs:
- out_tokens: bfloat16 [24, 400, 768], P('items', 'seq')
- grad_tokens: bfloat16 [24, 400, 768], P('items', 'seq')
- grad_ln1_gain: float32 [768], replicated
- grad_ln1_shift: float32 [768], replicated
- grad_w_query: float32 [768, 768], replicated
- grad_b_query: float32 [768], replicated
- grad_w_key: float32 [768, 768], replicated
- grad_w_value: float32 [768, 768], replicated
- grad_b_value: float32 [768], replicated
- grad_w_out: float32 [768, 768], replicated
- grad_b_out: float32 [768], replicated
- grad_ln2_gain: float32 [768], replicated
- grad_ln2_shift: float32 [768], replicated
- grad_w_inner: float32 [768, 3072], replicated
- grad_b_inner: float32 [3072], replicated
- grad_w_outer: float32 [3072, 768], replicated
- grad_b_outer: float32 [768], replicated
Inputs may be any that keep to these rules, and one draw needn't show every extreme that they name: `key_valid`: in each item the ones come first and the zeros last; an item has 1 to 3 zeros, and some item has exactly 3.
All inputs are finite; a program needn't handle non-finite values.
Results may differ from a plain program's by a relative error of at most 0.012.
The roundings to bfloat16 on the way count: a program that leaves them out, or rounds other values in their place, can miss the bound.
Values may be sent and summed in bfloat16 or wider, within the bound.
No kernel may reach another device: no remote copies, remote signals or barrier semaphores. Data moves between devices by JAX's collectives and lax.ppermute only.
A program may use at most 192 MiB of HBM per device.

v0:
```python
import jax
import jax.numpy as jnp
from jax import lax
from jax.sharding import PartitionSpec as P

D = 768
HEADS = 12
HEAD_DIM = 64
FF = 3072
EPSILON = 1e-06
MASKED = -1000000000.0


def norm_rows(values, gain, shift):
    center = values - jnp.mean(values, axis=-1, keepdims=True)
    spread = jnp.mean(center * center, axis=-1, keepdims=True)
    return center * lax.rsqrt(spread + EPSILON) * gain + shift


def gelu_exact(values):
    return jax.nn.gelu(values, approximate=False)


def flat_rows(values):
    return values.reshape(-1, values.shape[-1])


def tall_dot(left, right):
    return jnp.einsum(
        "ti,tj->ij", flat_rows(left), flat_rows(right), preferred_element_type=jnp.float32
    )


def wide_dot(left, weight):
    return jnp.dot(flat_rows(left), weight, preferred_element_type=jnp.float32)


def back_dot(grads, weight):
    return jnp.einsum("tj,ij->ti", flat_rows(grads), weight, preferred_element_type=jnp.float32)


def column_sum(values):
    return jnp.sum(flat_rows(values.astype(jnp.float32)), axis=0)


def attend_scores(queries, keysets, usable, factor):
    scores = (
        jnp.einsum("bqhd,bkhd->bhqk", queries, keysets, preferred_element_type=jnp.float32) * factor
    )
    return jnp.where(usable[:, None, None, :] > 0, scores, MASKED)


def local(
    tokens,
    cotangent,
    ln1_gain,
    ln1_shift,
    w_query,
    b_query,
    w_key,
    w_value,
    b_value,
    w_out,
    b_out,
    ln2_gain,
    ln2_shift,
    w_inner,
    b_inner,
    w_outer,
    b_outer,
    key_valid,
):
    groups = lax.axis_size("seq")
    item_count, row_count, model_width = tokens.shape
    length = row_count * groups
    heads_here = HEADS // groups
    factor = HEAD_DIM ** (-0.5)
    token_shape = (item_count, row_count, model_width)
    head_shape = (item_count, length, heads_here, HEAD_DIM)
    inputs = tokens.astype(jnp.float32)
    normed, first_pull = jax.vjp(
        norm_rows, inputs, ln1_gain.astype(jnp.float32), ln1_shift.astype(jnp.float32)
    )
    normed_low = normed.astype(jnp.bfloat16)
    query = (
        (wide_dot(normed_low, w_query) + b_query.astype(jnp.float32))
        .astype(jnp.bfloat16)
        .reshape(token_shape)
    )
    keyset = wide_dot(normed_low, w_key).astype(jnp.bfloat16).reshape(token_shape)
    values = (
        (wide_dot(normed_low, w_value) + b_value.astype(jnp.float32))
        .astype(jnp.bfloat16)
        .reshape(token_shape)
    )
    query_heads, key_heads, value_heads = (
        lax.all_to_all(query, "seq", split_axis=2, concat_axis=1, tiled=True),
        lax.all_to_all(keyset, "seq", split_axis=2, concat_axis=1, tiled=True),
        lax.all_to_all(values, "seq", split_axis=2, concat_axis=1, tiled=True),
    )
    query_four = query_heads.reshape(head_shape)
    key_four = key_heads.reshape(head_shape)
    value_four = value_heads.reshape(head_shape)
    scores = attend_scores(query_four, key_four, key_valid, factor)
    row_top = jnp.max(scores, axis=-1, keepdims=True)
    weights = jnp.exp(scores - row_top)
    totals = jnp.sum(weights, axis=-1, keepdims=True)
    logsum = row_top + jnp.log(totals)
    probs_low = (weights / totals).astype(jnp.bfloat16)
    mixed = jnp.einsum("bhqk,bkhd->bqhd", probs_low, value_four, preferred_element_type=jnp.float32)
    mixed = mixed.astype(jnp.bfloat16).reshape(item_count, length, heads_here * HEAD_DIM)
    mixed_tokens = lax.all_to_all(mixed, "seq", split_axis=1, concat_axis=2, tiled=True)
    hidden = inputs + wide_dot(mixed_tokens, w_out).reshape(token_shape) + b_out.astype(jnp.float32)
    normed_two, second_pull = jax.vjp(
        norm_rows, hidden, ln2_gain.astype(jnp.float32), ln2_shift.astype(jnp.float32)
    )
    normed_two_low = normed_two.astype(jnp.bfloat16)
    inner = (wide_dot(normed_two_low, w_inner) + b_inner.astype(jnp.float32)).reshape(
        item_count, row_count, FF
    )
    active, gelu_pull = jax.vjp(gelu_exact, inner)
    active_low = active.astype(jnp.bfloat16)
    result = (
        hidden + wide_dot(active_low, w_outer).reshape(token_shape) + b_outer.astype(jnp.float32)
    )
    out_tokens = result.astype(jnp.bfloat16)
    grad_w_outer = tall_dot(active_low, cotangent)
    grad_b_outer = column_sum(cotangent)
    d_active = back_dot(cotangent, w_outer).reshape(item_count, row_count, FF)
    (d_inner,) = gelu_pull(d_active)
    d_inner_low = d_inner.astype(jnp.bfloat16)
    grad_w_inner = tall_dot(normed_two_low, d_inner_low)
    grad_b_inner = column_sum(d_inner_low)
    d_normed_two = back_dot(d_inner_low, w_inner).reshape(token_shape)
    d_hidden_part, grad_ln2_gain, grad_ln2_shift = second_pull(d_normed_two)
    d_hidden = cotangent.astype(jnp.float32) + d_hidden_part
    grad_b_out = column_sum(d_hidden)
    d_hidden_low = d_hidden.astype(jnp.bfloat16)
    grad_w_out = tall_dot(mixed_tokens, d_hidden_low)
    d_mixed = back_dot(d_hidden_low, w_out).astype(jnp.bfloat16).reshape(token_shape)
    d_mixed_heads = lax.all_to_all(d_mixed, "seq", split_axis=2, concat_axis=1, tiled=True)
    d_mixed_four = d_mixed_heads.reshape(head_shape)
    scores = attend_scores(query_four, key_four, key_valid, factor)
    probs = jnp.exp(scores - logsum)
    d_value = jnp.einsum(
        "bhqk,bqhd->bkhd",
        probs.astype(jnp.bfloat16),
        d_mixed_four,
        preferred_element_type=jnp.float32,
    )
    d_probs = jnp.einsum(
        "bqhd,bkhd->bhqk", d_mixed_four, value_four, preferred_element_type=jnp.float32
    )
    weighted = jnp.sum(probs * d_probs, axis=-1, keepdims=True)
    d_scores = (probs * (d_probs - weighted)).astype(jnp.bfloat16)
    d_query = (
        jnp.einsum("bhqk,bkhd->bqhd", d_scores, key_four, preferred_element_type=jnp.float32)
        * factor
    )
    d_key = (
        jnp.einsum("bhqk,bqhd->bkhd", d_scores, query_four, preferred_element_type=jnp.float32)
        * factor
    )
    flat_shape = (item_count, length, heads_here * HEAD_DIM)
    d_query = d_query.astype(jnp.bfloat16).reshape(flat_shape)
    d_key = d_key.astype(jnp.bfloat16).reshape(flat_shape)
    d_value = d_value.astype(jnp.bfloat16).reshape(flat_shape)
    d_query_tok, d_key_tok, d_value_tok = (
        lax.all_to_all(d_query, "seq", split_axis=1, concat_axis=2, tiled=True),
        lax.all_to_all(d_key, "seq", split_axis=1, concat_axis=2, tiled=True),
        lax.all_to_all(d_value, "seq", split_axis=1, concat_axis=2, tiled=True),
    )
    grad_w_query = tall_dot(normed_low, d_query_tok)
    grad_b_query = column_sum(d_query_tok)
    grad_w_key = tall_dot(normed_low, d_key_tok)
    grad_w_value = tall_dot(normed_low, d_value_tok)
    grad_b_value = column_sum(d_value_tok)
    d_normed = (
        back_dot(d_query_tok, w_query) + back_dot(d_key_tok, w_key) + back_dot(d_value_tok, w_value)
    )
    d_input_part, grad_ln1_gain, grad_ln1_shift = first_pull(d_normed.reshape(token_shape))
    grad_tokens = (d_hidden + d_input_part).astype(jnp.bfloat16)
    smalls = jnp.concatenate(
        [
            grad_ln1_gain,
            grad_ln1_shift,
            grad_b_query,
            grad_b_value,
            grad_b_out,
            grad_ln2_gain,
            grad_ln2_shift,
            grad_b_outer,
            grad_b_inner,
        ]
    )
    flat_query = grad_w_query.reshape(-1)
    flat_key = grad_w_key.reshape(-1)
    flat_value = grad_w_value.reshape(-1)
    flat_out = grad_w_out.reshape(-1)
    flat_inner = grad_w_inner.reshape(-1)
    flat_outer = grad_w_outer.reshape(-1)
    shares = (
        lax.psum_scatter(flat_query, ("items", "seq"), scatter_dimension=0, tiled=True),
        lax.psum_scatter(flat_key, ("items", "seq"), scatter_dimension=0, tiled=True),
        lax.psum_scatter(flat_value, ("items", "seq"), scatter_dimension=0, tiled=True),
        lax.psum_scatter(flat_out, ("items", "seq"), scatter_dimension=0, tiled=True),
        lax.psum_scatter(flat_inner, ("items", "seq"), scatter_dimension=0, tiled=True),
        lax.psum_scatter(flat_outer, ("items", "seq"), scatter_dimension=0, tiled=True),
        lax.psum_scatter(smalls, ("items", "seq"), scatter_dimension=0, tiled=True),
    )
    summed = (
        lax.all_gather(shares[0].astype(jnp.bfloat16), ("items", "seq"), axis=0, tiled=True).astype(
            jnp.float32
        ),
        lax.all_gather(shares[1].astype(jnp.bfloat16), ("items", "seq"), axis=0, tiled=True).astype(
            jnp.float32
        ),
        lax.all_gather(shares[2].astype(jnp.bfloat16), ("items", "seq"), axis=0, tiled=True).astype(
            jnp.float32
        ),
        lax.all_gather(shares[3].astype(jnp.bfloat16), ("items", "seq"), axis=0, tiled=True).astype(
            jnp.float32
        ),
        lax.all_gather(shares[4].astype(jnp.bfloat16), ("items", "seq"), axis=0, tiled=True).astype(
            jnp.float32
        ),
        lax.all_gather(shares[5].astype(jnp.bfloat16), ("items", "seq"), axis=0, tiled=True).astype(
            jnp.float32
        ),
        lax.all_gather(shares[6].astype(jnp.bfloat16), ("items", "seq"), axis=0, tiled=True).astype(
            jnp.float32
        ),
    )
    sum_query, sum_key, sum_value, sum_out, sum_inner, sum_outer, sum_small = summed
    width = D
    return (
        out_tokens,
        grad_tokens,
        sum_small[0:width],
        sum_small[width : 2 * width],
        sum_query.reshape(D, D),
        sum_small[2 * width : 3 * width],
        sum_key.reshape(D, D),
        sum_value.reshape(D, D),
        sum_small[3 * width : 4 * width],
        sum_out.reshape(D, D),
        sum_small[4 * width : 5 * width],
        sum_small[5 * width : 6 * width],
        sum_small[6 * width : 7 * width],
        sum_inner.reshape(D, FF),
        sum_small[8 * width : 8 * width + FF],
        sum_outer.reshape(FF, D),
        sum_small[7 * width : 8 * width],
    )


def solution(mesh):
    in_specs = (
        P("items", "seq", None),
        P("items", "seq", None),
        P(),
        P(),
        P(),
        P(),
        P(),
        P(),
        P(),
        P(),
        P(),
        P(),
        P(),
        P(),
        P(),
        P(),
        P(),
        P("items", None),
    )
    out_specs = (
        P("items", "seq", None),
        P("items", "seq", None),
        P(),
        P(),
        P(),
        P(),
        P(),
        P(),
        P(),
        P(),
        P(),
        P(),
        P(),
        P(),
        P(),
        P(),
        P(),
    )
    return jax.shard_map(local, mesh=mesh, in_specs=in_specs, out_specs=out_specs, check_vma=False)
```

profile of v0, /device:TPU:0, one launch (start us, length us, event | category | flops | bytes accessed | tf_op | source)
XLA Modules:
  0.0 1186.7 jit_solution(8166704738698876618)
XLA Ops:
  16.3 6.3 all-to-all-start
  25.9 16.9 %all-to-all-done = bf16[3,100,768]{1,0,2:T(4,128)(2,1)S(1)} async-done(((bf16[3,100,768]{1,0,2:T(4,128)(2,1)}), bf16[3,100,768]{1,0,2:T(4,128)(2,1)S(1)}, u32[]{:S(2)}, u32[]{:S(2)}) %all-to-all-start) | async-done | bytes 460832 | tf_op jit(solution)/shard_map/all_to_all | solution.py:99
  52.9 13.0 %all-to-all-done.1 = bf16[3,100,768]{1,0,2:T(4,128)(2,1)S(1)} async-done(((bf16[3,100,768]{1,0,2:T(4,128)(2,1)}), bf16[3,100,768]{1,0,2:T(4,128)(2,1)S(1)}, u32[]{:S(2)}, u32[]{:S(2)}) %all-to-all-start.1) | async-done | bytes 460832 | tf_op jit(solution)/shard_map/all_to_all | solution.py:97
  65.9 4.2 all-to-all-start.2
  74.1 15.8 %all-to-all-done.2 = bf16[3,100,768]{1,0,2:T(4,128)(2,1)} async-done(((bf16[3,100,768]{1,0,2:T(4,128)(2,1)}), bf16[3,100,768]{1,0,2:T(4,128)(2,1)}, u32[]{:S(2)}, u32[]{:S(2)}) %all-to-all-start.2) | async-done | bytes 460832 | tf_op jit(solution)/shard_map/all_to_all | solution.py:98
  107.3 20.2 %all-to-all-done.3 = bf16[3,400,192]{2,0,1:T(4,128)(2,1)S(1)} async-done(((bf16[3,400,192]{2,0,1:T(4,128)(2,1)}), bf16[3,400,192]{2,0,1:T(4,128)(2,1)S(1)}, u32[]{:S(2)}, u32[]{:S(2)}) %all-to-all-start.3) | async-done | bytes 460832 | tf_op jit(solution)/shard_map/all_to_all | solution.py:112
  137.3 13.2 %negate_multiply_fusion = (f32[300,3072]{1,0:T(8,128)}, bf16[300,3072]{1,0:T(8,128)(2,1)}, f32[300,3072]{1,0:T(8,128)}) fusion(f32[3072]{0:T(1024)S(1)} %convert_element_type.162, bf16[300,768]{1,0:T(8,128)(2,1)} %reshape.289, bf16[768,3072]{1,0:T(8,128)(2,1)} %param.31), kind=kOutput, calls=%fused_computation.49 | convolution fusion | flops 1476403200 | bytes 14407680 | tf_op jit(solution)/shard_map/dot_general | solution.py:35
  158.1 13.9 %convert_reduce_fusion = (f32[3072]{0:T(1024)}, bf16[3,100,3072]{2,1,0:T(8,128)(2,1)S(1)}) fusion(f32[3,100,3072]{2,1,0:T(8,128)} %mul.183, f32[3,100,3072]{2,1,0:T(8,128)} %mul.179, bf16[3,100,768]{2,1,0:T(8,128)(2,1)} %param.19, bf16[3072,768]{1,0:T(8,128)(2,1)} %param.33), kind=kOutput, calls=%fused_computation.20 | convolution fusion | flops 1481008128 | bytes 14407680 | tf_op jit(solution)/shard_map/tj,ij->ti/dot_general | solution.py:39
  172.0 5.7 multiply_reduce_fusion.1
  185.2 4.7 all-to-all-start.4
  189.9 14.2 %convolution_bitcast_fusion = f32[3072,768]{1,0:T(8,128)} fusion(bf16[3,100,768]{2,1,0:T(8,128)(2,1)S(1)} %copy-done.24, f32[3,100,3072]{2,1,0:T(8,128)} %mul.179, f32[3,100,3072]{2,1,0:T(8,128)} %mul.183), kind=kOutput, calls=%fused_computation.8 | convolution fusion | flops 1472716800 | bytes 17270784 | tf_op jit(solution)/shard_map/ti,tj->ij/dot_general | solution.py:29
  215.4 5.5 multiply_reduce_fusion
  221.0 4.6 multiply_convert_fusion
  229.6 5.2 all-to-all-start.5
  234.8 4.4 convolution_bitcast_fusion.1
  239.2 5.9 copy.146
  245.1 10.8 reshape.316
  255.9 4.1 fusion.36
  262.2 5.1 all-to-all-start.6
  267.3 5.1 fusion.38
  279.1 7.6 all-to-all-done.6
  301.1 9.4 all-to-all-done.7
  357.3 460.4 %all-reduce.10 = (bf16[9216]{0:T(1024)(128)(2,1)}, bf16[589824]{0:T(1024)(128)(2,1)}, bf16[589824]{0:T(1024)(128)(2,1)}, bf16[589824]{0:T(1024)(128)(2,1)}, bf16...) all-reduce(f32[9216]{0:T(1024)} %constant_dynamic-update-slice_fusi, ...), channel_id=2, replica_groups=mesh['items'=8,'seq'=4] {'items','seq'}, use_global_device_ids=true, to_apply=%region_20.21.clone | all-reduce | flops 7087104 | bytes 42522624
  829.7 5.4 fusion.47
  836.0 37.5 %all-reduce = bf16[9216]{0:T(1024)(128)(2,1)S(1)} all-reduce(bf16[9216]{0:T(1024)(128)(2,1)S(1)} %dynamic-update-slice), channel_id=1, replica_groups=mesh['items'=8,'seq'=4] {'items','seq'}, use_global_device_ids=true, to_apply=%add | all-reduce | flops 9216 | bytes 36864
  878.1 49.6 %all-gather.9.cloned.1.call-done = bf16[589824]{0:T(1024)(128)(2,1)} async-done(((bf16[18432]{0:T(1024)(128)(2,1)}), bf16[589824]{0:T(1024)(128)(2,1)}) %all-gather.9.cloned.1.call-update) | async-done | bytes 1179664 | tf_op jit(solution)/shard_map/all_gather | solution.py:215
  931.0 52.4 %all-gather.11.cloned.1.call-done = bf16[589824]{0:T(1024)(128)(2,1)} async-done(((bf16[18432]{0:T(1024)(128)(2,1)}), bf16[589824]{0:T(1024)(128)(2,1)}) %all-gather.11.cloned.1.call-update) | async-done | bytes 1179664 | tf_op jit(solution)/shard_map/all_gather | solution.py:218
  986.8 52.3 %all-gather.13.cloned.1.call-done = bf16[589824]{0:T(1024)(128)(2,1)} async-done(((bf16[18432]{0:T(1024)(128)(2,1)}), bf16[589824]{0:T(1024)(128)(2,1)}) %all-gather.13.cloned.1.call-update) | async-done | bytes 1179664 | tf_op jit(solution)/shard_map/all_gather | solution.py:221
  1042.4 62.4 %all-gather.15.cloned.1.call-done = bf16[2359296]{0:T(1024)(128)(2,1)} async-done(((bf16[73728]{0:T(1024)(128)(2,1)}), bf16[2359296]{0:T(1024)(128)(2,1)}) %all-gather.15.cloned.1.call-update) | async-done | bytes 4718608 | tf_op jit(solution)/shard_map/all_gather | solution.py:224
  1104.8 8.7 reshape.328
  1113.6 55.8 %all-gather.17.cloned.1.call-done = bf16[2359296]{0:T(1024)(128)(2,1)} async-done(((bf16[73728]{0:T(1024)(128)(2,1)}), bf16[2359296]{0:T(1024)(128)(2,1)}) %all-gather.17.cloned.1.call-update) | async-done | bytes 4718608 | tf_op jit(solution)/shard_map/all_gather | solution.py:227
  1169.4 10.0 reshape.330
  (228 shorter events, 181.1 us)
Async XLA Ops:
  13.7 32.6 %copy-start.9 = (bf16[300,768]{1,0:T(8,128)(2,1)}, bf16[300,768]{1,0:T(8,128)(2,1)S(1)}, u32[]{:S(2)}) copy-start(bf16[300,768]{1,0:T(8,128)(2,1)S(1)} %reshape.281) | copy-start | bytes 1382404
  16.3 26.5 %all-to-all-start = ((bf16[3,100,768]{1,0,2:T(4,128)(2,1)}), bf16[3,100,768]{1,0,2:T(4,128)(2,1)S(1)}, u32[]{:S(2)}, u32[]{:S(2)}) async-start(bf16[3,100,768]{1,0,2:T(4,128)(2,1)} %copy.94), calls=%async_computation | async-start | bytes 1572864 | tf_op jit(solution)/shard_map/all_to_all | solution.py:99
  25.9 44.3 %copy-start.39 = (s32[3,400]{1,0:T(4,128)S(1)}, s32[3,400]{1,0:T(4,128)}, u32[]{:S(2)}) copy-start(s32[3,400]{1,0:T(4,128)} %param.35) | copy-start | bytes 14404
  42.8 23.1 %all-to-all-start.1 = ((bf16[3,100,768]{1,0,2:T(4,128)(2,1)}), bf16[3,100,768]{1,0,2:T(4,128)(2,1)S(1)}, u32[]{:S(2)}, u32[]{:S(2)}) async-start(bf16[3,100,768]{1,0,2:T(4,128)(2,1)} %copy.97), calls=%async_computation.1 | async-start | bytes 1572864 | tf_op jit(solution)/shard_map/all_to_all | solution.py:97
  65.9 23.9 %all-to-all-start.2 = ((bf16[3,100,768]{1,0,2:T(4,128)(2,1)}), bf16[3,100,768]{1,0,2:T(4,128)(2,1)}, u32[]{:S(2)}, u32[]{:S(2)}) async-start(bf16[3,100,768]{1,0,2:T(4,128)(2,1)} %copy.100), calls=%async_computation.2 | async-start | bytes 1572864 | tf_op jit(solution)/shard_map/all_to_all | solution.py:98
  73.2 24.8 %copy-start.20 = (bf16[3,400,3,64]{1,3,2,0:T(8,128)(2,1)}, bf16[3,400,3,64]{1,3,2,0:T(8,128)(2,1)S(1)}, u32[]{:S(2)}) copy-start(bf16[3,400,3,64]{1,3,2,0:T(8,128)(2,1)S(1)} %reshape.283) | copy-start | bytes 1382404
  98.0 9.2 copy-start.42
  98.0 9.3 copy-start.40
  98.0 9.3 copy-start.43
  98.0 9.3 copy-start.44
  101.2 30.9 %copy-start.3 = (bf16[3,100,768]{2,1,0:T(8,128)(2,1)S(1)}, bf16[3,100,768]{2,1,0:T(8,128)(2,1)}, u32[]{:S(2)}) copy-start(bf16[3,100,768]{2,1,0:T(8,128)(2,1)} %param.18) | copy-start | bytes 1382404
  103.5 24.0 %all-to-all-start.3 = ((bf16[3,400,192]{2,0,1:T(4,128)(2,1)}), bf16[3,400,192]{2,0,1:T(4,128)(2,1)S(1)}, u32[]{:S(2)}, u32[]{:S(2)}) async-start(bf16[3,400,192]{2,0,1:T(4,128)(2,1)} %copy.104), calls=%async_computation.3 | async-start | bytes 1638400 | tf_op jit(solution)/shard_map/all_to_all | solution.py:112
  107.3 113.7 %copy-start.28 = (f32[3,3,400]{2,1,0:T(4,128)}, f32[3,3,400]{2,1,0:T(4,128)S(1)}, u32[]{:S(2)}) copy-start(f32[3,3,400]{2,1,0:T(4,128)S(1)} %log_add_fusion) | copy-start | bytes 43204
  134.2 43.5 %copy-start.7 = (f32[3,100,768]{2,1,0:T(8,128)}, f32[3,100,768]{2,1,0:T(8,128)S(1)}, u32[]{:S(2)}) copy-start(f32[3,100,768]{2,1,0:T(8,128)S(1)} %get-tuple-element.48) | copy-start | bytes 2764804
  179.3 10.7 copy-start.24
  185.2 26.1 %all-to-all-start.4 = ((bf16[3,100,768]{1,0,2:T(4,128)(2,1)}), bf16[3,100,768]{1,0,2:T(4,128)(2,1)}, u32[]{:S(2)}, u32[]{:S(2)}) async-start(bf16[3,100,768]{1,0,2:T(4,128)(2,1)} %copy.107), calls=%async_computation.4 | async-start | bytes 1572864 | tf_op jit(solution)/shard_map/all_to_all | solution.py:141
  189.9 14.3 %copy-start.16 = (bf16[3,100,4,192]{3,2,1,0:T(4,128)(2,1)S(1)}, bf16[3,100,4,192]{3,2,1,0:T(4,128)(2,1)}, u32[]{:S(2)}) copy-start(bf16[3,100,4,192]{3,2,1,0:T(4,128)(2,1)} %copy-done.15) | copy-start | bytes 1382404
  229.6 32.6 %all-to-all-start.5 = ((bf16[3,400,192]{2,0,1:T(4,128)(2,1)}), bf16[3,400,192]{2,0,1:T(4,128)(2,1)S(1)}, u32[]{:S(2)}, u32[]{:S(2)}) async-start(bf16[3,400,192]{2,0,1:T(4,128)(2,1)} %copy.111), calls=%async_computation.5 | async-start | bytes 1638400 | tf_op jit(solution)/shard_map/all_to_all | solution.py:169
  255.9 11.4 copy-start.29
  262.2 11.6 copy-start.11
  262.2 24.5 %all-to-all-start.6 = ((bf16[3,400,192]{2,0,1:T(4,128)(2,1)}), bf16[3,400,192]{2,0,1:T(4,128)(2,1)}, u32[]{:S(2)}, u32[]{:S(2)}) async-start(bf16[3,400,192]{2,0,1:T(4,128)(2,1)} %copy.115), calls=%async_computation.6 | async-start | bytes 1638400 | tf_op jit(solution)/shard_map/all_to_all | solution.py:170
  286.7 23.8 %all-to-all-start.7 = ((bf16[3,400,192]{2,0,1:T(4,128)(2,1)}), bf16[3,400,192]{2,0,1:T(4,128)(2,1)S(1)}, u32[]{:S(2)}, u32[]{:S(2)}) async-start(bf16[3,400,192]{2,0,1:T(4,128)(2,1)} %copy.119), calls=%async_computation.7 | async-start | bytes 1638400 | tf_op jit(solution)/shard_map/all_to_all | solution.py:171
  290.2 584.5 %all-gather.7.cloned.1.call-start = ((), (), s32[]{:S(2)}) async-start(), calls=%async_computation.8 | async-start | bytes 1216512 | tf_op jit(solution)/shard_map/all_gather | solution.py:212
  322.6 14.8 %copy-start.38 = (f32[768]{0:T(1024)S(1)}, f32[768]{0:T(1024)}, u32[]{:S(2)}) copy-start(f32[768]{0:T(1024)} %get-tuple-element.19) | copy-start | bytes 9220
  322.6 26.5 %copy-start.5 = (f32[768,768]{1,0:T(8,128)S(1)}, f32[768,768]{1,0:T(8,128)}, u32[]{:S(2)}) copy-start(f32[768,768]{1,0:T(8,128)} %fusion.75) | copy-start | bytes 7077892
  357.3 469.6 %copy-start.45 = (bf16[768]{0:T(1024)(128)(2,1)S(1)}, bf16[768]{0:T(1024)(128)(2,1)}, u32[]{:S(2)}) copy-start(bf16[768]{0:T(1024)(128)(2,1)} %param.34) | copy-start | bytes 4612
  817.7 12.0 %copy-start.8 = (f32[3,100,768]{2,1,0:T(8,128)S(1)}, f32[3,100,768]{2,1,0:T(8,128)}, u32[]{:S(2)}) copy-start(f32[3,100,768]{2,1,0:T(8,128)} %copy-done.7) | copy-start | bytes 2764804
  819.2 108.5 %all-gather.9.cloned.1.call-start = ((), (), s32[]{:S(2)}) async-start(), calls=%async_computation.9 | async-start | bytes 1216512 | tf_op jit(solution)/shard_map/all_gather | solution.py:215
  820.6 162.8 %all-gather.11.cloned.1.call-start = ((), (), s32[]{:S(2)}) async-start(), calls=%async_computation.10 | async-start | bytes 1216512 | tf_op jit(solution)/shard_map/all_gather | solution.py:218
  822.1 216.9 %all-gather.13.cloned.1.call-start = ((), (), s32[]{:S(2)}) async-start(), calls=%async_computation.11 | async-start | bytes 1216512 | tf_op jit(solution)/shard_map/all_gather | solution.py:221
  823.6 281.3 %all-gather.15.cloned.1.call-start = ((), (), s32[]{:S(2)}) async-start(), calls=%async_computation.12 | async-start | bytes 4866048 | tf_op jit(solution)/shard_map/all_gather | solution.py:224
  825.2 344.2 %all-gather.17.cloned.1.call-start = ((), (), s32[]{:S(2)}) async-start(), calls=%async_computation.13 | async-start | bytes 4866048 | tf_op jit(solution)/shard_map/all_gather | solution.py:227
  (28 other events, 110.1 us)
Sparse Core Ops, SparseCore 0:
  819.3 52.1 all-gather.6
  874.9 52.7 all-gather.8
  930.5 52.9 all-gather.10
  986.1 52.8 all-gather.12
  1042.3 62.5 all-gather.14
  1107.5 61.8 all-gather.16
where the time goes:
time: 1200 us; the launch traced here: 1190 us
  blocking collectives  498 us (42%)
  waiting for transfers between devices  356 us (30%)
  local copies, waits for them, and re-layouts  156 us (13%)
  matrix products  103 us (9%)
  starting transfers between devices  36.5 us (3%)
  other arithmetic  22.6 us (2%)
  between operations  15.3 us (1%)
    unnamed x2, blocking collectives  498 us
    all_gather x1, waiting for transfers between devices, local(): lax.all_gather(shares[4].astype(jnp.bfloat16), ('items', 'seq'), axis=0,...  62.4 us
    all_gather x1, waiting for transfers between devices, local(): lax.all_gather(shares[5].astype(jnp.bfloat16), ('items', 'seq'), axis=0,...  55.8 us
    all_gather x1, waiting for transfers between devices, local(): lax.all_gather(shares[2].astype(jnp.bfloat16), ('items', 'seq'), axis=0,...  52.4 us
    all_gather x1, waiting for transfers between devices, local(): lax.all_gather(shares[3].astype(jnp.bfloat16), ('items', 'seq'), axis=0,...  52.3 us
    all_gather x1, waiting for transfers between devices, local(): lax.all_gather(shares[1].astype(jnp.bfloat16), ('items', 'seq'), axis=0,...  49.6 us
    unnamed x110, local copies, waits for them, and re-layouts  31.7 us
    dot_general x6, matrix products, tall_dot(): jnp.einsum('ti,tj->ij', flat_rows(left), flat_rows(right), preferred_elem...  28.5 us
  transfers between devices with their start and end apart: 14, of which 11 were waited for; matrix products, arithmetic and copies ran while one was open for 11% of the time, Pallas kernels for 0%

commit v1 on v0

--- a/solution.py
+++ b/solution.py
@@ -109,7 +109,10 @@
     probs_low = (weights / totals).astype(jnp.bfloat16)
     mixed = jnp.einsum("bhqk,bkhd->bqhd", probs_low, value_four, preferred_element_type=jnp.float32)
     mixed = mixed.astype(jnp.bfloat16).reshape(item_count, length, heads_here * HEAD_DIM)
-    mixed_tokens = lax.all_to_all(mixed, "seq", split_axis=1, concat_axis=2, tiled=True)
+    mixed_tokens = jnp.concatenate(
+        lax.all_to_all(jnp.stack(jnp.split(mixed, lax.axis_size("seq"), axis=1)), "seq", 0, 0),
+        axis=2,
+    )
     hidden = inputs + wide_dot(mixed_tokens, w_out).reshape(token_shape) + b_out.astype(jnp.float32)
     normed_two, second_pull = jax.vjp(
         norm_rows, hidden, ln2_gain.astype(jnp.float32), ln2_shift.astype(jnp.float32)

time: 1200 us -> 1190 us (level)
    unnamed x110 -> x108, local copies, waits for them, and re-layouts: 31.7 us -> 30.8 us
where the time goes in v1:
time: 1190 us; the launch traced here: 1180 us
  blocking collectives  498 us (42%)
  waiting for transfers between devices  350 us (29%)
  local copies, waits for them, and re-layouts  152 us (13%)
  matrix products  102 us (9%)
  starting transfers between devices  36.5 us (3%)
  other arithmetic  24.1 us (2%)
  between operations  15.4 us (1%)
    unnamed x2, blocking collectives  498 us
    all_gather x1, waiting for transfers between devices, local(): lax.all_gather(shares[4].astype(jnp.bfloat16), ('items', 'seq'), axis=0,...  62.4 us
    all_gather x1, waiting for transfers between devices, local(): lax.all_gather(shares[5].astype(jnp.bfloat16), ('items', 'seq'), axis=0,...  55.8 us
    all_gather x1, waiting for transfers between devices, local(): lax.all_gather(shares[2].astype(jnp.bfloat16), ('items', 'seq'), axis=0,...  52.4 us
    all_gather x1, waiting for transfers between devices, local(): lax.all_gather(shares[3].astype(jnp.bfloat16), ('items', 'seq'), axis=0,...  52.3 us
    all_gather x1, waiting for transfers between devices, local(): lax.all_gather(shares[1].astype(jnp.bfloat16), ('items', 'seq'), axis=0,...  49.6 us
    unnamed x108, local copies, waits for them, and re-layouts  30.8 us
    dot_general x6, matrix products, tall_dot(): jnp.einsum('ti,tj->ij', flat_rows(left), flat_rows(right), preferred_elem...  28.5 us
  transfers between devices with their start and end apart: 14, of which 11 were waited for; matrix products, arithmetic and copies ran while one was open for 11% of the time, Pallas kernels for 0%

profile of v1, /device:TPU:0, one launch (start us, length us, event | category | flops | bytes accessed | tf_op | source)
XLA Modules:
  0.0 1178.3 jit_solution(8481112149853781753)
XLA Ops:
  16.3 6.3 all-to-all-start
  25.9 16.9 %all-to-all-done = bf16[3,100,768]{1,0,2:T(4,128)(2,1)S(1)} async-done(((bf16[3,100,768]{1,0,2:T(4,128)(2,1)}), bf16[3,100,768]{1,0,2:T(4,128)(2,1)S(1)}, u32[]{:S(2)}, u32[]{:S(2)}) %all-to-all-start) | async-done | bytes 460832 | tf_op jit(solution)/shard_map/all_to_all | solution.py:99
  52.9 13.0 %all-to-all-done.1 = bf16[3,100,768]{1,0,2:T(4,128)(2,1)S(1)} async-done(((bf16[3,100,768]{1,0,2:T(4,128)(2,1)}), bf16[3,100,768]{1,0,2:T(4,128)(2,1)S(1)}, u32[]{:S(2)}, u32[]{:S(2)}) %all-to-all-start.1) | async-done | bytes 460832 | tf_op jit(solution)/shard_map/all_to_all | solution.py:97
  65.9 4.2 all-to-all-start.2
  74.1 15.8 %all-to-all-done.2 = bf16[3,100,768]{1,0,2:T(4,128)(2,1)} async-done(((bf16[3,100,768]{1,0,2:T(4,128)(2,1)}), bf16[3,100,768]{1,0,2:T(4,128)(2,1)}, u32[]{:S(2)}, u32[]{:S(2)}) %all-to-all-start.2) | async-done | bytes 460832 | tf_op jit(solution)/shard_map/all_to_all | solution.py:98
  106.0 14.7 %all-to-all-done.3 = bf16[4,3,100,192]{2,3,1,0:T(8,128)(2,1)S(1)} async-done(((bf16[4,3,100,192]{2,3,1,0:T(8,128)(2,1)}), bf16[4,3,100,192]{2,3,1,0:T(8,128)(2,1)S(1)}, u32[]{:S(2)}, u32[]{:S(2)}) %all-to-all-start.3) | async-done | bytes 460832 | tf_op jit(solution)/shard_map/all_to_all | solution.py:113
  128.8 13.2 %negate_multiply_fusion = (f32[300,3072]{1,0:T(8,128)}, bf16[300,3072]{1,0:T(8,128)(2,1)}, f32[300,3072]{1,0:T(8,128)}) fusion(f32[3072]{0:T(1024)S(1)} %convert_element_type.162, bf16[300,768]{1,0:T(8,128)(2,1)} %reshape.288, bf16[768,3072]{1,0:T(8,128)(2,1)} %param.31), kind=kOutput, calls=%fused_computation.49 | convolution fusion | flops 1476403200 | bytes 14407680 | tf_op jit(solution)/shard_map/dot_general | solution.py:35
  149.6 13.9 %convert_reduce_fusion = (f32[3072]{0:T(1024)}, bf16[3,100,3072]{2,1,0:T(8,128)(2,1)S(1)}) fusion(f32[3,100,3072]{2,1,0:T(8,128)} %mul.183, f32[3,100,3072]{2,1,0:T(8,128)} %mul.179, bf16[3,100,768]{2,1,0:T(8,128)(2,1)} %param.19, bf16[3072,768]{1,0:T(8,128)(2,1)} %param.33), kind=kOutput, calls=%fused_computation.20 | convolution fusion | flops 1481008128 | bytes 14407680 | tf_op jit(solution)/shard_map/tj,ij->ti/dot_general | solution.py:39
  163.6 5.7 multiply_reduce_fusion.1
  176.8 4.7 all-to-all-start.4
  181.5 14.2 %convolution_bitcast_fusion = f32[3072,768]{1,0:T(8,128)} fusion(bf16[3,100,768]{2,1,0:T(8,128)(2,1)S(1)} %copy-done.23, f32[3,100,3072]{2,1,0:T(8,128)} %mul.179, f32[3,100,3072]{2,1,0:T(8,128)} %mul.183), kind=kOutput, calls=%fused_computation.8 | convolution fusion | flops 1472716800 | bytes 17270784 | tf_op jit(solution)/shard_map/ti,tj->ij/dot_general | solution.py:29
  207.0 5.5 multiply_reduce_fusion
  212.6 4.6 multiply_convert_fusion
  221.1 5.2 all-to-all-start.5
  226.4 4.4 convolution_bitcast_fusion.1
  230.7 5.9 copy.143
  236.6 10.8 reshape.314
  247.5 4.0 fusion.36
  253.8 5.1 all-to-all-start.6
  258.9 5.1 fusion.38
  270.6 7.6 all-to-all-done.6
  292.7 9.4 all-to-all-done.7
  348.8 460.4 %all-reduce.10 = (bf16[9216]{0:T(1024)(128)(2,1)}, bf16[589824]{0:T(1024)(128)(2,1)}, bf16[589824]{0:T(1024)(128)(2,1)}, bf16[589824]{0:T(1024)(128)(2,1)}, bf16...) all-reduce(f32[9216]{0:T(1024)} %constant_dynamic-update-slice_fusi, ...), channel_id=2, replica_groups=mesh['items'=8,'seq'=4] {'items','seq'}, use_global_device_ids=true, to_apply=%region_20.21.clone | all-reduce | flops 7087104 | bytes 42522624
  821.2 5.4 fusion.47
  827.5 37.5 %all-reduce = bf16[9216]{0:T(1024)(128)(2,1)S(1)} all-reduce(bf16[9216]{0:T(1024)(128)(2,1)S(1)} %dynamic-update-slice), channel_id=1, replica_groups=mesh['items'=8,'seq'=4] {'items','seq'}, use_global_device_ids=true, to_apply=%add | all-reduce | flops 9216 | bytes 36864
  869.6 49.6 %all-gather.9.cloned.1.call-done = bf16[589824]{0:T(1024)(128)(2,1)} async-done(((bf16[18432]{0:T(1024)(128)(2,1)}), bf16[589824]{0:T(1024)(128)(2,1)}) %all-gather.9.cloned.1.call-update) | async-done | bytes 1179664 | tf_op jit(solution)/shard_map/all_gather | solution.py:218
  922.6 52.4 %all-gather.11.cloned.1.call-done = bf16[589824]{0:T(1024)(128)(2,1)} async-done(((bf16[18432]{0:T(1024)(128)(2,1)}), bf16[589824]{0:T(1024)(128)(2,1)}) %all-gather.11.cloned.1.call-update) | async-done | bytes 1179664 | tf_op jit(solution)/shard_map/all_gather | solution.py:221
  978.3 52.3 %all-gather.13.cloned.1.call-done = bf16[589824]{0:T(1024)(128)(2,1)} async-done(((bf16[18432]{0:T(1024)(128)(2,1)}), bf16[589824]{0:T(1024)(128)(2,1)}) %all-gather.13.cloned.1.call-update) | async-done | bytes 1179664 | tf_op jit(solution)/shard_map/all_gather | solution.py:224
  1033.9 62.4 %all-gather.15.cloned.1.call-done = bf16[2359296]{0:T(1024)(128)(2,1)} async-done(((bf16[73728]{0:T(1024)(128)(2,1)}), bf16[2359296]{0:T(1024)(128)(2,1)}) %all-gather.15.cloned.1.call-update) | async-done | bytes 4718608 | tf_op jit(solution)/shard_map/all_gather | solution.py:227
  1096.3 8.7 reshape.326
  1105.1 55.8 %all-gather.17.cloned.1.call-done = bf16[2359296]{0:T(1024)(128)(2,1)} async-done(((bf16[73728]{0:T(1024)(128)(2,1)}), bf16[2359296]{0:T(1024)(128)(2,1)}) %all-gather.17.cloned.1.call-update) | async-done | bytes 4718608 | tf_op jit(solution)/shard_map/all_gather | solution.py:230
  1160.9 10.0 reshape.328
  (227 shorter events, 178.1 us)
Async XLA Ops:
  13.6 9.1 copy-start.40
  13.7 32.6 %copy-start.9 = (bf16[300,768]{1,0:T(8,128)(2,1)}, bf16[300,768]{1,0:T(8,128)(2,1)S(1)}, u32[]{:S(2)}) copy-start(bf16[300,768]{1,0:T(8,128)(2,1)S(1)} %reshape.279) | copy-start | bytes 1382404
  16.3 26.5 %all-to-all-start = ((bf16[3,100,768]{1,0,2:T(4,128)(2,1)}), bf16[3,100,768]{1,0,2:T(4,128)(2,1)S(1)}, u32[]{:S(2)}, u32[]{:S(2)}) async-start(bf16[3,100,768]{1,0,2:T(4,128)(2,1)} %copy.96), calls=%async_computation | async-start | bytes 1572864 | tf_op jit(solution)/shard_map/all_to_all | solution.py:99
  25.9 44.3 %copy-start.38 = (s32[3,400]{1,0:T(4,128)S(1)}, s32[3,400]{1,0:T(4,128)}, u32[]{:S(2)}) copy-start(s32[3,400]{1,0:T(4,128)} %param.35) | copy-start | bytes 14404
  42.8 23.1 %all-to-all-start.1 = ((bf16[3,100,768]{1,0,2:T(4,128)(2,1)}), bf16[3,100,768]{1,0,2:T(4,128)(2,1)S(1)}, u32[]{:S(2)}, u32[]{:S(2)}) async-start(bf16[3,100,768]{1,0,2:T(4,128)(2,1)} %copy.99), calls=%async_computation.1 | async-start | bytes 1572864 | tf_op jit(solution)/shard_map/all_to_all | solution.py:97
  65.9 23.9 %all-to-all-start.2 = ((bf16[3,100,768]{1,0,2:T(4,128)(2,1)}), bf16[3,100,768]{1,0,2:T(4,128)(2,1)}, u32[]{:S(2)}, u32[]{:S(2)}) async-start(bf16[3,100,768]{1,0,2:T(4,128)(2,1)} %copy.102), calls=%async_computation.2 | async-start | bytes 1572864 | tf_op jit(solution)/shard_map/all_to_all | solution.py:98
  73.2 24.7 %copy-start.19 = (bf16[3,400,3,64]{1,3,2,0:T(8,128)(2,1)}, bf16[3,400,3,64]{1,3,2,0:T(8,128)(2,1)S(1)}, u32[]{:S(2)}) copy-start(bf16[3,400,3,64]{1,3,2,0:T(8,128)(2,1)S(1)} %reshape.281) | copy-start | bytes 1382404
  97.9 8.0 copy-start.39
  97.9 8.0 copy-start.42
  97.9 8.0 copy-start.43
  100.4 23.2 %copy-start.3 = (bf16[3,100,768]{2,1,0:T(8,128)(2,1)S(1)}, bf16[3,100,768]{2,1,0:T(8,128)(2,1)}, u32[]{:S(2)}) copy-start(bf16[3,100,768]{2,1,0:T(8,128)(2,1)} %param.18) | copy-start | bytes 1382404
  101.6 19.1 %all-to-all-start.3 = ((bf16[4,3,100,192]{2,3,1,0:T(8,128)(2,1)}), bf16[4,3,100,192]{2,3,1,0:T(8,128)(2,1)S(1)}, u32[]{:S(2)}, u32[]{:S(2)}) async-start(bf16[4,3,100,192]{2,3,1,0:T(8,128)(2,1)} %pad_maximum_fusion), calls=%async_computation.3 | async-start | bytes 1179648 | tf_op jit(solution)/shard_map/all_to_all | solution.py:113
  106.0 106.5 %copy-start.27 = (f32[3,3,400]{2,1,0:T(4,128)}, f32[3,3,400]{2,1,0:T(4,128)S(1)}, u32[]{:S(2)}) copy-start(f32[3,3,400]{2,1,0:T(4,128)S(1)} %log_add_fusion) | copy-start | bytes 43204
  125.7 43.6 %copy-start.7 = (f32[3,100,768]{2,1,0:T(8,128)}, f32[3,100,768]{2,1,0:T(8,128)S(1)}, u32[]{:S(2)}) copy-start(f32[3,100,768]{2,1,0:T(8,128)S(1)} %get-tuple-element.52) | copy-start | bytes 2764804
  170.8 10.6 copy-start.23
  176.8 26.1 %all-to-all-start.4 = ((bf16[3,100,768]{1,0,2:T(4,128)(2,1)}), bf16[3,100,768]{1,0,2:T(4,128)(2,1)}, u32[]{:S(2)}, u32[]{:S(2)}) async-start(bf16[3,100,768]{1,0,2:T(4,128)(2,1)} %copy.107), calls=%async_computation.4 | async-start | bytes 1572864 | tf_op jit(solution)/shard_map/all_to_all | solution.py:144
  181.4 14.3 %copy-start.16 = (bf16[3,100,4,192]{3,2,1,0:T(4,128)(2,1)S(1)}, bf16[3,100,4,192]{3,2,1,0:T(4,128)(2,1)}, u32[]{:S(2)}) copy-start(bf16[3,100,4,192]{3,2,1,0:T(4,128)(2,1)} %copy-done.15) | copy-start | bytes 1382404
  221.1 32.6 %all-to-all-start.5 = ((bf16[3,400,192]{2,0,1:T(4,128)(2,1)}), bf16[3,400,192]{2,0,1:T(4,128)(2,1)S(1)}, u32[]{:S(2)}, u32[]{:S(2)}) async-start(bf16[3,400,192]{2,0,1:T(4,128)(2,1)} %copy.111), calls=%async_computation.5 | async-start | bytes 1638400 | tf_op jit(solution)/shard_map/all_to_all | solution.py:172
  247.5 11.4 copy-start.28
  253.8 11.6 copy-start.11
  253.8 24.5 %all-to-all-start.6 = ((bf16[3,400,192]{2,0,1:T(4,128)(2,1)}), bf16[3,400,192]{2,0,1:T(4,128)(2,1)}, u32[]{:S(2)}, u32[]{:S(2)}) async-start(bf16[3,400,192]{2,0,1:T(4,128)(2,1)} %copy.115), calls=%async_computation.6 | async-start | bytes 1638400 | tf_op jit(solution)/shard_map/all_to_all | solution.py:173
  278.2 23.8 %all-to-all-start.7 = ((bf16[3,400,192]{2,0,1:T(4,128)(2,1)}), bf16[3,400,192]{2,0,1:T(4,128)(2,1)S(1)}, u32[]{:S(2)}, u32[]{:S(2)}) async-start(bf16[3,400,192]{2,0,1:T(4,128)(2,1)} %copy.119), calls=%async_computation.7 | async-start | bytes 1638400 | tf_op jit(solution)/shard_map/all_to_all | solution.py:174
  281.7 584.5 %all-gather.7.cloned.1.call-start = ((), (), s32[]{:S(2)}) async-start(), calls=%async_computation.8 | async-start | bytes 1216512 | tf_op jit(solution)/shard_map/all_gather | solution.py:215
  314.2 14.8 %copy-start.37 = (f32[768]{0:T(1024)S(1)}, f32[768]{0:T(1024)}, u32[]{:S(2)}) copy-start(f32[768]{0:T(1024)} %get-tuple-element.19) | copy-start | bytes 9220
  314.2 26.5 %copy-start.5 = (f32[768,768]{1,0:T(8,128)S(1)}, f32[768,768]{1,0:T(8,128)}, u32[]{:S(2)}) copy-start(f32[768,768]{1,0:T(8,128)} %fusion.75) | copy-start | bytes 7077892
  348.8 469.6 %copy-start.44 = (bf16[768]{0:T(1024)(128)(2,1)S(1)}, bf16[768]{0:T(1024)(128)(2,1)}, u32[]{:S(2)}) copy-start(bf16[768]{0:T(1024)(128)(2,1)} %param.34) | copy-start | bytes 4612
  809.2 12.0 %copy-start.8 = (f32[3,100,768]{2,1,0:T(8,128)S(1)}, f32[3,100,768]{2,1,0:T(8,128)}, u32[]{:S(2)}) copy-start(f32[3,100,768]{2,1,0:T(8,128)} %copy-done.7) | copy-start | bytes 2764804
  810.7 108.5 %all-gather.9.cloned.1.call-start = ((), (), s32[]{:S(2)}) async-start(), calls=%async_computation.9 | async-start | bytes 1216512 | tf_op jit(solution)/shard_map/all_gather | solution.py:218
  812.2 162.8 %all-gather.11.cloned.1.call-start = ((), (), s32[]{:S(2)}) async-start(), calls=%async_computation.10 | async-start | bytes 1216512 | tf_op jit(solution)/shard_map/all_gather | solution.py:221
  813.6 217.0 %all-gather.13.cloned.1.call-start = ((), (), s32[]{:S(2)}) async-start(), calls=%async_computation.11 | async-start | bytes 1216512 | tf_op jit(solution)/shard_map/all_gather | solution.py:224
  815.1 281.3 %all-gather.15.cloned.1.call-start = ((), (), s32[]{:S(2)}) async-start(), calls=%async_computation.12 | async-start | bytes 4866048 | tf_op jit(solution)/shard_map/all_gather | solution.py:227
  816.7 344.2 %all-gather.17.cloned.1.call-start = ((), (), s32[]{:S(2)}) async-start(), calls=%async_computation.13 | async-start | bytes 4866048 | tf_op jit(solution)/shard_map/all_gather | solution.py:230
  (27 other events, 106.9 us)
Sparse Core Ops, SparseCore 0:
  810.8 52.1 all-gather.6
  866.4 52.7 all-gather.8
  922.0 52.9 all-gather.10
  977.6 52.8 all-gather.12
  1033.8 62.5 all-gather.14
  1099.0 61.8 all-gather.16
